TPU v7x, 256 devices: a whole 4x4x8 slice. The times are simulated.
256 devices in a mesh: row: 8 (over z_lo, y), col: 16 (over z_hi, x), leaf: 2 (over core).
Axes of the slice: x: 4, y: 4, z: 8 (z_hi: 4, z_lo: 2; z = z_hi * 2 + z_lo), core: 2. Of those that a mesh axis runs over, the one named last changes fastest.
Arguments:
- front: float32 [16384, 16384], P('row', ('col', 'leaf')), may hold values from -6 to 6
- child: float32 [16384, 16384], P(('row', 'col', 'leaf')), may hold values from -6 to 6
- row_map: int32 [8, 8], P('row'), may hold values from 0 to 7, each once within a row
- col_map: int32 [64], replicated, may hold values from 0 to 63, each once
- x_fac: float32 [64, 16384], P('row', ('col', 'leaf')), may hold values from -0.75 to 0.75
- w_fac: float32 [64, 16384], P('row', ('col', 'leaf')), may hold values from -0.375 to 0.375
- v_fac: float32 [64, 16384], P(('col', 'leaf'), 'row'), may hold values from -6 to 6
- z_fac: float32 [64, 16384], P(('col', 'leaf'), 'row'), may hold values from -0.75 to 0.75
- dinv: float32 [256, 256], replicated, may hold values from -0.375 to 0.375
- pivots: int32 [256], replicated, may hold values from 0 to 255, each once
- rank_rows: int32 [64], P('row'), may hold values from 16 to 64
- rank_cols: int32 [64], P(('col', 'leaf')), may hold values from 16 to 64
- admissible: int32 [64, 64], P('row', ('col', 'leaf')), may hold values 0 or 1
Outputs:
- updated: float32 [16384, 16384], P('row', ('col', 'leaf'))
Inputs may be any that keep to these rules, and one draw needn't show every extreme that they name: Each row of row_map orders the 8 tile rows of one group; col_map orders all 64 tile columns. `pivots`: A permutation of the panel's columns.
All inputs are finite; a program needn't handle non-finite values. No bound on the sum of `admissible` on one device may be relied on, other than what follows from the above.
Results may differ from a plain program's by a relative error of at most 0.0003.
Values sent between devices are 32-bit elements; how exact they have to be, the bound alone decides.
A program may use at most 128 MiB of HBM per device.

v0:
```python
import jax
import jax.numpy as jnp
from jax import lax
from jax.sharding import PartitionSpec as P

RMAX = 64


def inverse_order(order):
    count = order.shape[0]
    return jnp.zeros((count,), jnp.int32).at[order].set(jnp.arange(count, dtype=jnp.int32))


def on_device(
    front,
    child,
    row_map,
    col_map,
    x_fac,
    w_fac,
    v_fac,
    z_fac,
    dinv,
    pivots,
    rank_rows,
    rank_cols,
    admissible,
):
    highest = lax.Precision.HIGHEST
    tile = dinv.shape[0]
    row_tiles = front.shape[0] // tile
    col_tiles = front.shape[1] // tile
    col_width = front.shape[1]
    all_cols = col_map.shape[0]
    local_rows = child.shape[0]
    col_count = lax.axis_size("col")
    leaf_count = lax.axis_size("leaf")
    placed = jnp.take(child.reshape(local_rows, all_cols, tile), inverse_order(col_map), axis=1)
    outbound = placed.reshape(1, local_rows, col_count * leaf_count, col_width)
    arrived = lax.all_to_all(outbound, ("col", "leaf"), split_axis=2, concat_axis=0, tiled=True)
    grouped = arrived.reshape(row_tiles, tile, col_width)
    relaid = jnp.take(grouped, inverse_order(row_map[0]), axis=0).reshape(
        row_tiles * tile, col_width
    )
    x_whole, w_whole = (
        lax.all_gather(x_fac, ("col", "leaf"), axis=1, tiled=True),
        lax.all_gather(w_fac, ("col", "leaf"), axis=1, tiled=True),
    )
    v_whole, z_whole = (
        lax.all_gather(v_fac, "row", axis=1, tiled=True),
        lax.all_gather(z_fac, "row", axis=1, tiled=True),
    )
    x_three = x_whole.reshape(row_tiles, RMAX, tile)
    w_three = w_whole.reshape(row_tiles, RMAX, tile)
    v_three = v_whole.reshape(col_tiles, RMAX, tile)
    z_three = z_whole.reshape(col_tiles, RMAX, tile)
    dv = jnp.einsum("kb,jrb->jkr", dinv, v_three, precision=highest)
    permuted = jnp.take(w_three, pivots, axis=2)
    core = jnp.einsum("irk,jks->ijrs", permuted, dv, precision=highest)
    rank_index = jnp.arange(RMAX, dtype=jnp.int32)
    dense_tile = (admissible == 0)[:, :, None]
    keep_rows = (rank_index[None, None, :] < rank_rows[:, None, None]) | dense_tile
    keep_cols = (rank_index[None, None, :] < rank_cols[None, :, None]) | dense_tile
    core = jnp.where(keep_rows[:, :, :, None] & keep_cols[:, :, None, :], core, jnp.float32(0.0))
    left = jnp.einsum("irb,ijrs->ibjs", x_three, core, precision=highest)
    update = jnp.einsum("ibjs,jsc->ibjc", left, z_three, precision=highest).reshape(
        row_tiles * tile, col_width
    )
    return front + relaid - update


def solution(mesh):
    return jax.shard_map(
        on_device,
        mesh=mesh,
        in_specs=(
            P("row", ("col", "leaf")),
            P(("row", "col", "leaf"), None),
            P("row", None),
            P(),
            P("row", ("col", "leaf")),
            P("row", ("col", "leaf")),
            P(("col", "leaf"), "row"),
            P(("col", "leaf"), "row"),
            P(),
            P(),
            P("row"),
            P(("col", "leaf")),
            P("row", ("col", "leaf")),
        ),
        out_specs=P("row", ("col", "leaf")),
        check_vma=False,
    )
```

profile of v0, /device:TPU:1, one launch (start us, length us, event | category | flops | bytes accessed | tf_op | source)
XLA Modules:
  0.0 322.9 jit_solution(7695282449139520069)
XLA Ops:
  0.0 0.7 compare_select_fusion.2
  0.7 0.8 scatter_custom_fusion.1
  1.5 4.8 %copy.71 = f32[8,64,8,256]{3,2,0,1:T(8,128)} copy(f32[8,64,8,256]{3,2,1,0:T(8,128)} %bitcast.71) | data formatting | bytes 8388608 | tf_op jit(solution)/shard_map/reshape | solution.py:38
  6.3 4.9 %gather_fusion = f32[64,64,256]{2,1,0:T(8,128)} fusion(f32[64,64,256]{2,0,1:T(8,128)} %bitcast.69, s32[1024]{0:T(1024)S(1)} %pad_clamp_fusion.2), kind=kCustom, calls=%fused_computation | custom fusion | bytes 8388864 | tf_op jit(solution)/shard_map/jit(_take)/gather | solution.py:38
  11.3 6.6 %copy.32 = f32[64,64,256]{2,1,0:T(8,128)} copy(f32[64,64,256]{2,0,1:T(8,128)} %bitcast.67) | data formatting | bytes 8388608 | tf_op jit(solution)/shard_map/jit(_take)/gather | solution.py:38
  17.9 5.2 %gather.17 = f32[1,64,32,512]{3,2,1,0:T(8,128)} reshape(f32[64,64,256]{2,1,0:T(8,128)} %copy.32) | data formatting | bytes 8388608 | tf_op jit(solution)/shard_map/jit(_take)/gather | solution.py:38
  23.1 0.1 broadcast_in_dim.65
  23.2 0.1 broadcast_in_dim.66
  23.4 2.8 broadcast_select_fusion
  26.2 4.4 %copy.33 = f32[1,64,32,512]{3,1,0,2:T(8,128)} copy(f32[1,64,32,512]{3,2,1,0:T(8,128)S(1)} %broadcast_select_fusion) | data formatting | bytes 8388608 | tf_op jit(solution)/shard_map/jit(_take)/select_n | solution.py:38
  30.6 12.8 %all-to-all-start = ((f32[1,64,32,512]{3,1,0,2:T(8,128)}), f32[1,64,32,512]{3,1,0,2:T(8,128)}, u32[]{:S(2)}, u32[]{:S(2)}) async-start(f32[1,64,32,512]{3,1,0,2:T(8,128)} %copy.33), calls=%async_computation | async-start | bytes 8388608 | tf_op jit(solution)/shard_map/all_to_all | solution.py:40
  43.4 0.1 copy.36
  43.5 129.5 %all_gather.13 = f32[8,16384]{1,0:T(8,128)S(1)} all-gather(f32[8,512]{1,0:T(8,128)S(1)} %copy-done.2), channel_id=1, replica_groups=mesh['row'=8,'col'=16,'leaf'=2] {'col','leaf'}, dimensions={1}, use_global_device_ids=true | all-gather | bytes 540672 | tf_op jit(solution)/shard_map/all_gather | solution.py:47
  173.0 0.2 copy.72
  173.2 0.4 copy.37
  173.6 1.0 gather_fusion.2
  174.7 22.0 %all_gather.12 = f32[2,16384]{1,0:T(2,128)S(1)} all-gather(f32[2,2048]{1,0:T(2,128)S(1)} %copy-done.3), channel_id=1, replica_groups=mesh['row'=8,'col'=16,'leaf'=2] {'row'}, dimensions={1}, use_global_device_ids=true | all-gather | bytes 147456 | tf_op jit(solution)/shard_map/all_gather | solution.py:50
  196.7 21.8 %all_gather.15 = f32[2,16384]{1,0:T(2,128)S(1)} all-gather(f32[2,2048]{1,0:T(2,128)S(1)} %copy-done.4), channel_id=1, replica_groups=mesh['row'=8,'col'=16,'leaf'=2] {'row'}, dimensions={1}, use_global_device_ids=true | all-gather | bytes 147456 | tf_op jit(solution)/shard_map/all_gather | solution.py:51
  218.5 0.4 convolution_bitcast_fusion.3
  219.1 54.4 %all_gather.14 = f32[8,16384]{1,0:T(8,128)S(1)} all-gather(f32[8,512]{1,0:T(8,128)S(1)} %copy-done.5), channel_id=1, replica_groups=mesh['row'=8,'col'=16,'leaf'=2] {'col','leaf'}, dimensions={1}, use_global_device_ids=true | all-gather | bytes 540672 | tf_op jit(solution)/shard_map/all_gather | solution.py:46
  273.5 0.3 select_bitcast_fusion
  273.9 0.9 fusion
  274.8 1.1 convolution_bitcast_fusion.1
  275.9 5.0 %convolution_bitcast_fusion = f32[8,256,2,256]{3,1,0,2:T(8,128)} fusion(f32[8,256,2,64]{1,3,0,2:T(8,128)S(1)} %convolution_bitcast_fusion.1, f32[1,2,64,256]{3,1,2,0:T(2,128)S(1)} %bitcast.76), kind=kOutput, calls=%fused_computation.7 | convolution fusion | flops 805306368 | bytes 5373952 | tf_op jit(solution)/shard_map/ibjs,jsc->ibjc/dot_general | solution.py:66
  280.9 5.5 %copy.40 = f32[8,256,2,256]{1,0,3,2:T(8,128)} copy(f32[8,256,2,256]{3,1,0,2:T(8,128)} %convolution_bitcast_fusion) | data formatting | bytes 8388608 | tf_op jit(solution)/shard_map/ibjs,jsc->ibjc/transpose | solution.py:66
  286.4 6.2 %copy.52 = f32[64,8,8,256]{3,1,2,0:T(8,128)} copy(f32[64,8,8,256]{3,2,1,0:T(8,128)} %bitcast.70) | data formatting | bytes 8388608
  292.6 0.6 scatter_custom_fusion
  293.3 5.4 %copy.35 = f32[2048,512]{0,1:T(8,128)} copy(f32[2048,512]{1,0:T(8,128)} %param.13) | data formatting | bytes 8388608 | tf_op args[0]
  298.7 5.0 %gather_fusion.1 = f32[8,256,512]{2,1,0:T(8,128)} fusion(f32[8,256,512]{2,1,0:T(8,128)} %bitcast.5, s32[1024]{0:T(1024)S(1)} %pad_clamp_fusion.1), kind=kCustom, calls=%fused_computation.1 | custom fusion | bytes 8388640 | tf_op jit(solution)/shard_map/jit(_take)/gather | solution.py:42
  303.7 5.4 %copy.34 = f32[2048,512]{0,1:T(8,128)} copy(f32[2048,512]{1,0:T(8,128)} %bitcast.68) | data formatting | bytes 8388608 | tf_op jit(solution)/shard_map/jit(_take)/gather | solution.py:42
  309.1 8.5 %add_subtract_fusion = f32[2048,512]{0,1:T(8,128)} fusion(f32[2048,512]{0,1:T(8,128)} %bitcast.66, f32[2048,512]{0,1:T(8,128)} %copy.35, f32[2048,512]{0,1:T(8,128)} %copy.34, pred[2048]{0:T(1024)(128)(4,1)S(1)} %broadcast_in_dim.62), kind=kLoop, calls=%fused_computation.6 | loop fusion | flops 3145728 | bytes 16779264 | tf_op jit(solution)/shard_map/sub | solution.py:69
  317.5 5.3 %copy.41 = f32[2048,512]{1,0:T(8,128)} copy(f32[2048,512]{0,1:T(8,128)} %add_subtract_fusion) | data formatting | bytes 8388608 | tf_op jit(solution)/shard_map/sub | solution.py:69
  (42 shorter events, 0.4 us)
Async XLA Ops:
  0.0 218.5 %copy-start = (f32[256,256]{1,0:T(8,128)S(1)}, f32[256,256]{1,0:T(8,128)}, u32[]{:S(2)}) copy-start(f32[256,256]{1,0:T(8,128)} %param.21) | copy-start | bytes 786436
  30.6 12.8 %copy-start.7 = (s32[8,2]{0,1:T(2,128)S(1)}, s32[8,2]{0,1:T(2,128)}, u32[]{:S(2)}) copy-start(s32[8,2]{0,1:T(2,128)} %param.25) | copy-start | bytes 196
  30.6 13.0 %copy-start.2 = (f32[8,512]{1,0:T(8,128)S(1)}, f32[8,512]{1,0:T(8,128)}, u32[]{:S(2)}) copy-start(f32[8,512]{1,0:T(8,128)} %param.18) | copy-start | bytes 49156
  30.6 143.0 %copy-start.6 = (s32[256]{0:T(256)S(1)}, s32[256]{0:T(256)}, u32[]{:S(2)}) copy-start(s32[256]{0:T(256)} %param.22) | copy-start | bytes 3076
  30.6 268.2 %all-to-all-start = ((f32[1,64,32,512]{3,1,0,2:T(8,128)}), f32[1,64,32,512]{3,1,0,2:T(8,128)}, u32[]{:S(2)}, u32[]{:S(2)}) async-start(f32[1,64,32,512]{3,1,0,2:T(8,128)} %copy.33), calls=%async_computation | async-start | bytes 8388608 | tf_op jit(solution)/shard_map/all_to_all | solution.py:40
  43.4 131.3 %copy-start.3 = (f32[2,2048]{1,0:T(2,128)S(1)}, f32[2,2048]{1,0:T(2,128)}, u32[]{:S(2)}) copy-start(f32[2,2048]{1,0:T(2,128)} %param.19) | copy-start | bytes 49156
  43.4 153.3 %copy-start.4 = (f32[2,2048]{1,0:T(2,128)S(1)}, f32[2,2048]{1,0:T(2,128)}, u32[]{:S(2)}) copy-start(f32[2,2048]{1,0:T(2,128)} %param.20) | copy-start | bytes 49156
  43.4 175.5 %copy-start.8 = (s32[2]{0:T(128)S(1)}, s32[2]{0:T(128)}, u32[]{:S(2)}) copy-start(s32[2]{0:T(128)} %param.24) | copy-start | bytes 28
  43.4 175.6 %copy-start.9 = (s32[8]{0:T(128)S(1)}, s32[8]{0:T(128)}, u32[]{:S(2)}) copy-start(s32[8]{0:T(128)} %param.23) | copy-start | bytes 100
  43.4 175.7 %copy-start.5 = (f32[8,512]{1,0:T(8,128)S(1)}, f32[8,512]{1,0:T(8,128)}, u32[]{:S(2)}) copy-start(f32[8,512]{1,0:T(8,128)} %param.17) | copy-start | bytes 49156
  286.4 6.2 %copy-start.10 = (s32[1,8]{1,0:T(1,128)S(1)}, s32[1,8]{1,0:T(1,128)}, u32[]{:S(2)}) copy-start(s32[1,8]{1,0:T(1,128)} %param.15) | copy-start | bytes 100
  309.1 13.8 %copy-start.1 = (f32[256,256]{1,0:T(8,128)S(1)}, f32[256,256]{1,0:T(8,128)}, u32[]{:S(2)}) copy-start(f32[256,256]{1,0:T(8,128)} %param.21) | copy-start | bytes 786436
where the time goes:
time: 324 us; the launch traced here: 323 us
  blocking collectives  228 us (70%)
  local copies, waits for them, and re-layouts  62.2 us (19%)
  starting transfers between devices  12.8 us (4%)
  other arithmetic  12.6 us (4%)
  matrix products  7.41 us (2%)
    all_gather x1, blocking collectives, on_device(): lax.all_gather(w_fac, ('col', 'leaf'), axis=1, tiled=True)  129 us
    all_gather x1, blocking collectives, on_device(): lax.all_gather(x_fac, ('col', 'leaf'), axis=1, tiled=True)  54.4 us
    all_gather x1, blocking collectives, on_device(): lax.all_gather(v_fac, 'row', axis=1, tiled=True)  22 us
    all_gather x1, blocking collectives, on_device(): lax.all_gather(z_fac, 'row', axis=1, tiled=True)  21.8 us
    gather x3, local copies, waits for them, and re-layouts, on_device(): jnp.take(child.reshape(local_rows, all_cols, tile), inverse_order(col_map...  16.8 us
    all_to_all x1, starting transfers between devices, on_device(): lax.all_to_all(outbound, ('col', 'leaf'), split_axis=2, concat_axis=0, ti...  12.8 us
    unnamed x26, local copies, waits for them, and re-layouts  11.8 us
    gather x2, local copies, waits for them, and re-layouts, on_device(): jnp.take(grouped, inverse_order(row_map[0]), axis=0)  10.3 us
  transfers between devices with their start and end apart: 1, of which 0 were waited for; matrix products, arithmetic and copies ran while one was open for 9% of the time, Pallas kernels for 0%

commit v1 on v0

v1 whole, which is shorter than its diff:
```python
import jax
import jax.numpy as jnp
from jax import lax
from jax.experimental import pallas as pl
from jax.experimental.pallas import tpu as pltpu
from jax.sharding import PartitionSpec as P

TILE = 256
RMAX = 64
MESH = pl.DeviceIdType.MESH
HIGHEST = lax.Precision.HIGHEST


def peer_of(row, col, leaf):
    return {"row": row, "col": col, "leaf": leaf}


def exchange_kernel(
    inv_col_h,
    rank_rows_h,
    rank_cols_h,
    admissible_h,
    child,
    front,
    x_fac_h,
    w_fac_h,
    v_fac_h,
    z_fac_h,
    dinv_h,
    pivots_h,
    arrived,
    front_v,
    inv_col,
    rank_rows,
    rank_cols,
    admissible,
    x_fac,
    w_fac,
    v_fac,
    z_fac,
    dinv,
    pivots,
    child_v,
    out_v,
    xw,
    vz,
    v_cat,
    z_diag,
    dv,
    local_sem,
    small_sem,
    a2a_send,
    a2a_recv,
    xw_send,
    xw_recv,
    vz_send,
    vz_recv,
):
    row, col, leaf = lax.axis_index("row"), lax.axis_index("col"), lax.axis_index("leaf")
    z_low, y = row // 4, row % 4
    z_high, x = col // 4, col % 4
    me = col * 2 + leaf

    def load_tile(c, carry):
        tile = child.at[:, pl.ds(pl.multiple_of(c * TILE, TILE), TILE)]
        pltpu.make_async_copy(tile, child_v.at[c], local_sem.at[0]).start()
        return carry

    load_front = pltpu.make_async_copy(front, front_v, local_sem.at[1])
    small = [
        pltpu.make_async_copy(source, target, small_sem.at[k])
        for k, (source, target) in enumerate(
            (
                (inv_col_h, inv_col),
                (x_fac_h, x_fac),
                (w_fac_h, w_fac),
                (v_fac_h, v_fac),
                (z_fac_h, z_fac),
                (dinv_h, dinv),
                (pivots_h, pivots),
                (rank_rows_h, rank_rows),
                (rank_cols_h, rank_cols),
                (admissible_h, admissible),
            )
        )
    ]
    for copy in small[:5]:
        copy.start()
    lax.fori_loop(0, 64, load_tile, 0)
    for copy in small[5:]:
        copy.start()

    barrier = pltpu.get_barrier_semaphore()

    def greet(m, carry):
        to = peer_of(
            row,
            ((z_high + m // 8) % 4) * 4 + (x + (m // 2) % 4) % 4,
            (leaf + m % 2) % 2,
        )
        pl.semaphore_signal(barrier, inc=1, device_id=to, device_id_type=MESH)
        return carry

    lax.fori_loop(1, 32, greet, 0)
    pl.semaphore_signal(
        barrier, inc=1, device_id=peer_of((1 - z_low) * 4 + y, col, leaf), device_id_type=MESH
    )
    for step in range(1, 4):
        pl.semaphore_signal(
            barrier,
            inc=1,
            device_id=peer_of(z_low * 4 + (y + step) % 4, col, leaf),
            device_id_type=MESH,
        )

    for copy in small[:5]:
        copy.wait()
    spot = leaf * 16 + x * 4 + z_high
    for c in range(4):
        lanes = slice(c * 128, (c + 1) * 128)
        xw[pl.ds(pl.multiple_of(spot * 64 + c * 16, 16), 8), :] = x_fac[:, lanes]
        xw[pl.ds(pl.multiple_of(spot * 64 + c * 16 + 8, 8), 8), :] = w_fac[:, lanes]
    place = y * 2 + z_low
    for q in range(8):
        lanes = slice(q * TILE, (q + 1) * TILE)
        for j in range(2):
            vz[place, 0, j, q : q + 1, :] = v_fac[j : j + 1, lanes]
            vz[place, 1, j, q : q + 1, :] = z_fac[j : j + 1, lanes]

    pl.semaphore_wait(barrier, 35)

    def xw_copy(start, count, stage, to):
        part = xw.at[pl.ds(pl.multiple_of(start * 64, 64), count * 64), :]
        return pltpu.make_async_remote_copy(
            src_ref=part,
            dst_ref=part,
            send_sem=xw_send.at[stage],
            recv_sem=xw_recv.at[stage],
            device_id=to,
            device_id_type=MESH,
        )

    def vz_copy(start, count, stage, to):
        part = vz.at[pl.ds(start, count)]
        return pltpu.make_async_remote_copy(
            src_ref=part,
            dst_ref=part,
            send_sem=vz_send.at[stage],
            recv_sem=vz_recv.at[stage],
            device_id=to,
            device_id_type=MESH,
        )

    xw_z = [
        xw_copy(spot, 1, 0, peer_of(row, ((z_high + s) % 4) * 4 + x, leaf)) for s in (2, 1, 3)
    ]
    xw_x = [
        xw_copy(leaf * 16 + x * 4, 4, 1, peer_of(row, z_high * 4 + (x + s) % 4, leaf))
        for s in (2, 1, 3)
    ]
    xw_leaf = [xw_copy(leaf * 16, 16, 2, peer_of(row, col, 1 - leaf))]
    vz_z = [vz_copy(place, 1, 0, peer_of((1 - z_low) * 4 + y, col, leaf))]
    vz_y = [
        vz_copy(y * 2, 2, 1, peer_of(z_low * 4 + (y + s) % 4, col, leaf)) for s in (2, 1, 3)
    ]

    for copy in xw_z + vz_z:
        copy.start()
    pltpu.make_async_copy(child_v, child_v, local_sem.at[0]).wait()
    load_front.start()

    def place_tiles(slot):
        for half in range(2):
            source = inv_col[slot * 2 + half]
            out_v[slot, :, half * TILE : (half + 1) * TILE] = child_v[source]

    def block_copy(m, dz):
        z_to, x_to, leaf_to = (z_high + dz) % 4, (x + m // 2) % 4, (leaf + m % 2) % 2
        slot = (z_to * 4 + x_to) * 2 + leaf_to
        return slot, pltpu.make_async_remote_copy(
            src_ref=out_v.at[slot],
            dst_ref=arrived.at[me],
            send_sem=a2a_send,
            recv_sem=a2a_recv,
            device_id=peer_of(row, z_to * 4 + x_to, leaf_to),
            device_id_type=MESH,
        )

    def send_blocks(first, dz):
        def one(m, carry):
            slot, copy = block_copy(m, dz)
            place_tiles(slot)
            copy.start()
            return carry

        lax.fori_loop(first, 8, one, 0)

    def settle_xw(pieces, stage):
        xw_copy(0, pieces, stage, peer_of(row, col, 1 - leaf)).wait()

    def settle_vz(pieces, stage):
        vz_copy(0, pieces, stage, peer_of(row, col, 1 - leaf)).wait()

    send_blocks(0, 2)
    settle_xw(3, 0)
    settle_vz(1, 0)
    for copy in xw_x + vz_y:
        copy.start()
    send_blocks(0, 1)
    settle_xw(12, 1)
    settle_vz(6, 1)
    for copy in xw_leaf:
        copy.start()
    send_blocks(0, 3)
    send_blocks(1, 0)
    place_tiles(me)
    arrived[me] = out_v[me]
    for copy in small[5:]:
        copy.wait()

    places = lax.broadcasted_iota(jnp.int32, (TILE, TILE), 0)
    chosen = jnp.where(places == pivots[...], jnp.float32(1.0), jnp.float32(0.0))
    permuted = jnp.dot(chosen, dinv[...], precision=HIGHEST, preferred_element_type=jnp.float32)
    z_diag[...] = jnp.zeros_like(z_diag)
    for j in range(2):
        for g in range(8):
            at = (g % 4) * 2 + g // 4
            v_cat[j * RMAX + g * 8 : j * RMAX + g * 8 + 8, :] = vz[at, 0, j]
            z_diag[j * RMAX + g * 8 : j * RMAX + g * 8 + 8, j * TILE : (j + 1) * TILE] = vz[
                at, 1, j
            ]
    dv[...] = lax.dot_general(
        permuted,
        v_cat[...],
        (((1,), (1,)), ((), ())),
        precision=HIGHEST,
        preferred_element_type=jnp.float32,
    )

    settle_xw(16, 2)
    load_front.wait()

    at = lax.broadcasted_iota(jnp.int32, (RMAX, 2 * RMAX), 0)
    piece = at % 32
    rank_row = (piece % 4) * 16 + ((piece // 4) % 4) * 4 + (piece // 16) * 2 + at // 32
    lane = lax.broadcasted_iota(jnp.int32, (RMAX, 2 * RMAX), 1)
    rank_col = lane % RMAX
    second = lane >= RMAX
    limit_col = jnp.where(second, rank_cols[1], rank_cols[0])

    def gathered(first):
        parts = [xw[pl.ds(first + c * 16, 32, stride=64), :] for c in range(4)]
        return jnp.concatenate(
            [jnp.concatenate(parts[:2], axis=1), jnp.concatenate(parts[2:], axis=1)], axis=0
        )

    def tile_row(i, carry):
        x_rows, w_rows = gathered(i), gathered(i + 8)
        core = jnp.dot(w_rows, dv[...], precision=HIGHEST, preferred_element_type=jnp.float32)
        dense = jnp.where(second, admissible[1, i], admissible[0, i]) == 0
        keep = dense | ((rank_row < rank_rows[i]) & (rank_col < limit_col))
        kept = jnp.where(keep, core, jnp.float32(0.0))
        left = lax.dot_general(
            x_rows,
            kept,
            (((0,), (0,)), ((), ())),
            precision=HIGHEST,
            preferred_element_type=jnp.float32,
        )
        update = jnp.dot(
            left, z_diag[...], precision=HIGHEST, preferred_element_type=jnp.float32
        )
        rows = pl.ds(pl.multiple_of(i * TILE, TILE), TILE)
        front_v[rows, :] = front_v[rows, :] - update
        return carry

    lax.fori_loop(0, 8, tile_row, 0)

    pltpu.make_async_remote_copy(
        src_ref=out_v.at[pl.ds(0, 31)],
        dst_ref=arrived.at[pl.ds(0, 31)],
        send_sem=a2a_send,
        recv_sem=a2a_recv,
        device_id=peer_of(row, col, 1 - leaf),
        device_id_type=MESH,
    ).wait()


def add_kernel(row_map, partial, arrived, updated):
    t = pl.program_id(0)
    source = 0
    for a in range(8):
        source = source + jnp.where(row_map[0, a] == t, a, 0)
    updated[...] = (
        partial[pl.ds(pl.multiple_of(t * TILE, TILE), TILE), :]
        + arrived[pl.ds(pl.multiple_of(source * TILE, TILE), TILE), :]
    )


def on_device(
    front,
    child,
    row_map,
    col_map,
    x_fac,
    w_fac,
    v_fac,
    z_fac,
    dinv,
    pivots,
    rank_rows,
    rank_cols,
    admissible,
):
    tiles = col_map.shape[0]
    order = jnp.arange(tiles, dtype=jnp.int32)
    inv_col = jnp.sum(
        jnp.where(col_map[None, :] == order[:, None], order[None, :], 0), axis=1, dtype=jnp.int32
    )
    vmem = pl.BlockSpec(memory_space=pltpu.VMEM)
    hbm = pl.BlockSpec(memory_space=pltpu.HBM)
    f32 = jnp.float32
    arrived, partial = pl.pallas_call(
        exchange_kernel,
        name="exchange",
        out_shape=(
            jax.ShapeDtypeStruct((32, 64, 512), f32),
            jax.ShapeDtypeStruct(front.shape, f32),
        ),
        in_specs=[hbm] * 12,
        out_specs=(vmem, vmem),
        scratch_shapes=[
            pltpu.SMEM((tiles,), jnp.int32),
            pltpu.SMEM(rank_rows.shape, jnp.int32),
            pltpu.SMEM(rank_cols.shape, jnp.int32),
            pltpu.SMEM(admissible.shape[::-1], jnp.int32),
            pltpu.VMEM(x_fac.shape, f32),
            pltpu.VMEM(w_fac.shape, f32),
            pltpu.VMEM(v_fac.shape, f32),
            pltpu.VMEM(z_fac.shape, f32),
            pltpu.VMEM(dinv.shape, f32),
            pltpu.VMEM((1, TILE), jnp.int32),
            pltpu.VMEM((tiles, child.shape[0], TILE), f32),
            pltpu.VMEM((32, 64, 512), f32),
            pltpu.VMEM((32 * 64, 128), f32),
            pltpu.VMEM((8, 2, 2, 8, TILE), f32),
            pltpu.VMEM((2 * RMAX, TILE), f32),
            pltpu.VMEM((2 * RMAX, 2 * TILE), f32),
            pltpu.VMEM((TILE, 2 * RMAX), f32),
            pltpu.SemaphoreType.DMA((2,)),
            pltpu.SemaphoreType.DMA((10,)),
            pltpu.SemaphoreType.DMA,
            pltpu.SemaphoreType.DMA,
            pltpu.SemaphoreType.DMA((3,)),
            pltpu.SemaphoreType.DMA((3,)),
            pltpu.SemaphoreType.DMA((2,)),
            pltpu.SemaphoreType.DMA((2,)),
        ],
        compiler_params=pltpu.CompilerParams(
            collective_id=0, has_side_effects=True, vmem_limit_bytes=32 << 20
        ),
    )(*(pltpu.with_memory_space_constraint(a, pltpu.HBM) for a in (
        inv_col,
        rank_rows,
        rank_cols,
        admissible.T,
        child,
        front,
        x_fac,
        w_fac,
        v_fac,
        z_fac,
        dinv,
        pivots.reshape(1, TILE),
    )))

    block = (TILE, 512)
    return pl.pallas_call(
        add_kernel,
        name="extend_add",
        out_shape=jax.ShapeDtypeStruct(front.shape, f32),
        grid_spec=pltpu.PrefetchScalarGridSpec(
            num_scalar_prefetch=1,
            grid=(8,),
            in_specs=[vmem, vmem],
            out_specs=pl.BlockSpec(block, lambda t, mapping: (t, 0)),
        ),
        compiler_params=pltpu.CompilerParams(vmem_limit_bytes=8 << 20),
        cost_estimate=pl.CostEstimate(
            flops=1 << 20, bytes_accessed=12 << 20, transcendentals=0
        ),
    )(row_map, partial, arrived.reshape(front.shape))


def solution(mesh):
    return jax.shard_map(
        on_device,
        mesh=mesh,
        in_specs=(
            P("row", ("col", "leaf")),
            P(("row", "col", "leaf"), None),
            P("row", None),
            P(),
            P("row", ("col", "leaf")),
            P("row", ("col", "leaf")),
            P(("col", "leaf"), "row"),
            P(("col", "leaf"), "row"),
            P(),
            P(),
            P("row"),
            P(("col", "leaf")),
            P("row", ("col", "leaf")),
        ),
        out_specs=P("row", ("col", "leaf")),
        check_vma=False,
    )
```

time: 324 us -> 114 us (0.35)
  blocking collectives: 228 us -> 0 us
  Pallas kernels: 0 us -> 112 us
  local copies, waits for them, and re-layouts: 62.2 us -> 0.01 us
  starting transfers between devices: 12.8 us -> 0 us
  other arithmetic: 12.6 us -> 1.28 us
  matrix products: 7.41 us -> 0 us
    all_gather x4 -> x0, blocking collectives: 228 us -> none  [the longest x1 129 us: on_device(): lax.all_gather(w_fac, ('col', 'leaf'), axis=1, tiled=True)]
    pallas_call x0 -> x2, Pallas kernels: none -> 112 us  [the longest x1 108 us: on_device(): pl.pallas_call(exchange_kernel, name='exchange', out_shape=(jax.ShapeDtyp...]
    gather x6 -> x0, local copies, waits for them, and re-layouts: 28.2 us -> none  [the longest x3 16.8 us: on_device(): jnp.take(child.reshape(local_rows, all_cols, tile), inverse_order(col_map...]
    all_to_all x1 -> x0, starting transfers between devices: 12.8 us -> none  [on_device(): lax.all_to_all(outbound, ('col', 'leaf'), split_axis=2, concat_axis=0, ti...]
    unnamed x26 -> x2, local copies, waits for them, and re-layouts: 11.8 us -> 0.01 us
    sub x1 -> x0, other arithmetic: 8.46 us -> none  [on_device(): return front + relaid - update]
    dot_general x4 -> x0, matrix products: 7.41 us -> none  [the longest x1 5.04 us: on_device(): jnp.einsum('ibjs,jsc->ibjc', left, z_three, precision=highest)]
    transpose x1 -> x0, local copies, waits for them, and re-layouts: 5.48 us -> none  [on_device(): jnp.einsum('ibjs,jsc->ibjc', left, z_three, precision=highest)]
  transfers between devices with their start and end apart: 1 -> 0, of which waited for: 0 -> 0; matrix products, arithmetic and copies ran while one was open for 9% -> 0% of each run, Pallas kernels for 0% -> 0%
where the time goes in v1:
time: 114 us
  Pallas kernels  112 us (98%)
  other arithmetic  1.28 us (1%)
    pallas_call x1, Pallas kernels, on_device(): pl.pallas_call(exchange_kernel, name='exchange', out_shape=(jax.ShapeDtyp...  108 us
    pallas_call x1, Pallas kernels, on_device(): pl.pallas_call(add_kernel, name='extend_add', out_shape=jax.ShapeDtypeStr...  4.13 us

profile of v1, /device:TPU:1, one launch (start us, length us, event | category | flops | bytes accessed | tf_op | source)
XLA Modules:
  0.0 113.8 jit_solution(3300777419127451383)
XLA Ops:
  0.0 1.3 %select_reduce_fusion.inv_col_h = s32[64]{0:T(128)} fusion(s32[64]{0:T(128)} %param.16), kind=kLoop, calls=%fused_computation | loop fusion | flops 12224 | bytes 512 | tf_op jit(solution)/shard_map/reduce_sum | solution.py:317
  1.3 0.0 copy-start
  1.3 108.3 %exchange.1 = (f32[32,64,512]{2,1,0:T(8,128)S(1)}, f32[2048,512]{1,0:T(8,128)S(1)}) custom-call(s32[64]{0:T(128)} %select_reduce_fusion.inv_col_h, s32[8]{0:T(128)} %rank_rows_h.1, s32[2]{0:T(128)} %rank_cols_h.1, s32[2,8]{1,0:T(2,128)} %bitcast.4, f32[64,16384]{1,0:T(8,128)} %child.1, f32[2048,512]{1,0:T(8,128)} %front.1, f32[8,512]{1,0:T(8,128)} %x_fac_h.1, ...), custom_call_target="tpu_custom_call" | custom-call | tf_op jit(solution)/shard_map/exchange/pallas_call | solution.py:323
  109.6 0.0 copy-done
  109.6 4.1 %extend_add.1 = f32[2048,512]{1,0:T(8,128)} custom-call(s32[1,8]{1,0:T(1,128)S(1)} %copy-done, f32[2048,512]{1,0:T(8,128)S(1)} %get-tuple-element.7.partial, f32[2048,512]{1,0:T(8,128)S(1)} %bitcast.3), custom_call_target="tpu_custom_call" | custom-call | flops 1048576 | bytes 12582912 | tf_op jit(solution)/shard_map/extend_add/pallas_call | solution.py:378
Async XLA Ops:
  1.3 108.3 %copy-start = (s32[1,8]{1,0:T(1,128)S(1)}, s32[1,8]{1,0:T(1,128)}, u32[]{:S(2)}) copy-start(s32[1,8]{1,0:T(1,128)} %row_map.1) | copy-start | bytes 100

commit v2 on v1

--- a/solution.py
+++ b/solution.py
@@ -16,7 +16,8 @@
 
 
 def exchange_kernel(
-    inv_col_h,
+    col_map_h,
+    row_map_h,
     rank_rows_h,
     rank_cols_h,
     admissible_h,
@@ -29,8 +30,8 @@
     dinv_h,
     pivots_h,
     arrived,
-    front_v,
-    inv_col,
+    col_map,
+    row_map,
     rank_rows,
     rank_cols,
     admissible,
@@ -42,6 +43,7 @@
     pivots,
     child_v,
     out_v,
+    front_v,
     xw,
     vz,
     v_cat,
@@ -71,7 +73,7 @@
         pltpu.make_async_copy(source, target, small_sem.at[k])
         for k, (source, target) in enumerate(
             (
-                (inv_col_h, inv_col),
+                (col_map_h, col_map),
                 (x_fac_h, x_fac),
                 (w_fac_h, w_fac),
                 (v_fac_h, v_fac),
@@ -81,15 +83,10 @@
                 (rank_rows_h, rank_rows),
                 (rank_cols_h, rank_cols),
                 (admissible_h, admissible),
+                (row_map_h, row_map),
             )
         )
     ]
-    for copy in small[:5]:
-        copy.start()
-    lax.fori_loop(0, 64, load_tile, 0)
-    for copy in small[5:]:
-        copy.start()
-
     barrier = pltpu.get_barrier_semaphore()
 
     def greet(m, carry):
@@ -112,6 +109,12 @@
             device_id=peer_of(z_low * 4 + (y + step) % 4, col, leaf),
             device_id_type=MESH,
         )
+
+    for copy in small[:5]:
+        copy.start()
+    lax.fori_loop(0, 64, load_tile, 0)
+    for copy in small[5:]:
+        copy.start()
 
     for copy in small[:5]:
         copy.wait()
@@ -170,8 +173,12 @@
     load_front.start()
 
     def place_tiles(slot):
-        for half in range(2):
-            source = inv_col[slot * 2 + half]
+        def find(b, found):
+            to = col_map[b]
+            return tuple(jnp.where(to == slot * 2 + h, b, found[h]) for h in range(2))
+
+        sources = lax.fori_loop(0, 64, find, (0, 0), unroll=8)
+        for half, source in enumerate(sources):
             out_v[slot, :, half * TILE : (half + 1) * TILE] = child_v[source]
 
     def block_copy(m, dz):
@@ -270,8 +277,8 @@
         update = jnp.dot(
             left, z_diag[...], precision=HIGHEST, preferred_element_type=jnp.float32
         )
-        rows = pl.ds(pl.multiple_of(i * TILE, TILE), TILE)
-        front_v[rows, :] = front_v[rows, :] - update
+        rows = pl.ds(i * 4, 4)
+        front_v[rows] = front_v[rows] - update.reshape(4, TILE // 4, 2 * TILE)
         return carry
 
     lax.fori_loop(0, 8, tile_row, 0)
@@ -285,16 +292,25 @@
         device_id_type=MESH,
     ).wait()
 
-
-def add_kernel(row_map, partial, arrived, updated):
-    t = pl.program_id(0)
-    source = 0
     for a in range(8):
-        source = source + jnp.where(row_map[0, a] == t, a, 0)
-    updated[...] = (
-        partial[pl.ds(pl.multiple_of(t * TILE, TILE), TILE), :]
-        + arrived[pl.ds(pl.multiple_of(source * TILE, TILE), TILE), :]
-    )
+        to = row_map[0, a]
+        for k in range(4):
+            arrived[a * 4 + k] = arrived[a * 4 + k] + front_v[to * 4 + k]
+
+
+def place_kernel(row_map, summed, updated, sem):
+    copies = []
+    for a in range(8):
+        rows = pl.ds(pl.multiple_of(row_map[0, a] * TILE, TILE), TILE)
+        copies.append(
+            pltpu.make_async_copy(
+                summed.at[a * TILE : (a + 1) * TILE], updated.at[rows], sem.at[a]
+            )
+        )
+    for copy in copies:
+        copy.start()
+    for copy in copies:
+        copy.wait()
 
 
 def on_device(
@@ -313,24 +329,18 @@
     admissible,
 ):
     tiles = col_map.shape[0]
-    order = jnp.arange(tiles, dtype=jnp.int32)
-    inv_col = jnp.sum(
-        jnp.where(col_map[None, :] == order[:, None], order[None, :], 0), axis=1, dtype=jnp.int32
-    )
     vmem = pl.BlockSpec(memory_space=pltpu.VMEM)
     hbm = pl.BlockSpec(memory_space=pltpu.HBM)
     f32 = jnp.float32
-    arrived, partial = pl.pallas_call(
+    summed = pl.pallas_call(
         exchange_kernel,
         name="exchange",
-        out_shape=(
-            jax.ShapeDtypeStruct((32, 64, 512), f32),
-            jax.ShapeDtypeStruct(front.shape, f32),
-        ),
-        in_specs=[hbm] * 12,
-        out_specs=(vmem, vmem),
+        out_shape=jax.ShapeDtypeStruct((32, 64, 512), f32),
+        in_specs=[hbm] * 13,
+        out_specs=vmem,
         scratch_shapes=[
             pltpu.SMEM((tiles,), jnp.int32),
+            pltpu.SMEM(row_map.shape, jnp.int32),
             pltpu.SMEM(rank_rows.shape, jnp.int32),
             pltpu.SMEM(rank_cols.shape, jnp.int32),
             pltpu.SMEM(admissible.shape[::-1], jnp.int32),
@@ -342,13 +352,14 @@
             pltpu.VMEM((1, TILE), jnp.int32),
             pltpu.VMEM((tiles, child.shape[0], TILE), f32),
             pltpu.VMEM((32, 64, 512), f32),
+            pltpu.VMEM((32, 64, 512), f32),
             pltpu.VMEM((32 * 64, 128), f32),
             pltpu.VMEM((8, 2, 2, 8, TILE), f32),
             pltpu.VMEM((2 * RMAX, TILE), f32),
             pltpu.VMEM((2 * RMAX, 2 * TILE), f32),
             pltpu.VMEM((TILE, 2 * RMAX), f32),
             pltpu.SemaphoreType.DMA((2,)),
-            pltpu.SemaphoreType.DMA((10,)),
+            pltpu.SemaphoreType.DMA((11,)),
             pltpu.SemaphoreType.DMA,
             pltpu.SemaphoreType.DMA,
             pltpu.SemaphoreType.DMA((3,)),
@@ -360,12 +371,13 @@
             collective_id=0, has_side_effects=True, vmem_limit_bytes=32 << 20
         ),
     )(*(pltpu.with_memory_space_constraint(a, pltpu.HBM) for a in (
-        inv_col,
+        col_map,
+        row_map,
         rank_rows,
         rank_cols,
         admissible.T,
         child,
-        front,
+        front.reshape(32, 64, 512),
         x_fac,
         w_fac,
         v_fac,
@@ -374,22 +386,15 @@
         pivots.reshape(1, TILE),
     )))
 
-    block = (TILE, 512)
     return pl.pallas_call(
-        add_kernel,
-        name="extend_add",
+        place_kernel,
+        name="place_rows",
         out_shape=jax.ShapeDtypeStruct(front.shape, f32),
-        grid_spec=pltpu.PrefetchScalarGridSpec(
-            num_scalar_prefetch=1,
-            grid=(8,),
-            in_specs=[vmem, vmem],
-            out_specs=pl.BlockSpec(block, lambda t, mapping: (t, 0)),
-        ),
+        in_specs=[pl.BlockSpec(memory_space=pltpu.SMEM), vmem],
+        out_specs=hbm,
+        scratch_shapes=[pltpu.SemaphoreType.DMA((8,))],
         compiler_params=pltpu.CompilerParams(vmem_limit_bytes=8 << 20),
-        cost_estimate=pl.CostEstimate(
-            flops=1 << 20, bytes_accessed=12 << 20, transcendentals=0
-        ),
-    )(row_map, partial, arrived.reshape(front.shape))
+    )(row_map, summed.reshape(front.shape))
 
 
 def solution(mesh):

time: 114 us -> 111 us (0.974)
  other arithmetic: 1.28 us -> 0 us
    pallas_call x2, Pallas kernels: 112 us -> 111 us  [the longest x1 108 us: on_device(): pl.pallas_call(exchange_kernel, name='exchange', out_shape=jax.ShapeDtype...]
    reduce_sum x1 -> x0, other arithmetic: 1.28 us -> none  [on_device(): jnp.sum(jnp.where(col_map[None, :] == order[:, None], order[None, :], 0),...]
where the time goes in v2:
time: 111 us
  Pallas kernels  111 us (100%)
    pallas_call x1, Pallas kernels, on_device(): pl.pallas_call(exchange_kernel, name='exchange', out_shape=jax.ShapeDtype...  108 us
    pallas_call x1, Pallas kernels, on_device(): pl.pallas_call(place_kernel, name='place_rows', out_shape=jax.ShapeDtypeS...  2.61 us

profile of v2, /device:TPU:1, one launch (start us, length us, event | category | flops | bytes accessed | tf_op | source)
XLA Modules:
  0.0 110.9 jit_solution(14642147233263722477)
XLA Ops:
  0.0 0.0 copy-start
  0.0 108.3 %exchange.1 = f32[32,64,512]{2,1,0:T(8,128)S(1)} custom-call(s32[64]{0:T(128)} %col_map_h.1, s32[1,8]{1,0:T(1,128)} %row_map.1, s32[8]{0:T(128)} %rank_rows_h.1, s32[2]{0:T(128)} %rank_cols_h.1, s32[2,8]{1,0:T(2,128)} %bitcast.6, f32[64,16384]{1,0:T(8,128)} %child.1, f32[32,64,512]{2,1,0:T(8,128)} %bitcast.5, f32[8,512]{1,0:T(8,128)} %x_fac_h.1, ...), custom_call_target="tpu_custom_call" | custom-call | tf_op jit(solution)/shard_map/exchange/pallas_call | solution.py:335
  108.3 0.0 copy-done
  108.3 2.6 %place_rows.1 = f32[2048,512]{1,0:T(8,128)} custom-call(s32[1,8]{1,0:T(1,128)S(1)} %copy-done, f32[2048,512]{1,0:T(8,128)S(1)} %bitcast.4), custom_call_target="tpu_custom_call" | custom-call | tf_op jit(solution)/shard_map/place_rows/pallas_call | solution.py:389
Async XLA Ops:
  0.0 108.3 %copy-start = (s32[1,8]{1,0:T(1,128)S(1)}, s32[1,8]{1,0:T(1,128)}, u32[]{:S(2)}) copy-start(s32[1,8]{1,0:T(1,128)} %row_map.1) | copy-start | bytes 100

commit v3 on v2

--- a/solution.py
+++ b/solution.py
@@ -8,6 +8,7 @@
 TILE = 256
 RMAX = 64
 MESH = pl.DeviceIdType.MESH
+PARTS = 2
 HIGHEST = lax.Precision.HIGHEST
 
 
@@ -30,6 +31,7 @@
     dinv_h,
     pivots_h,
     arrived,
+    front_v,
     col_map,
     row_map,
     rank_rows,
@@ -43,7 +45,6 @@
     pivots,
     child_v,
     out_v,
-    front_v,
     xw,
     vz,
     v_cat,
@@ -292,23 +293,14 @@
         device_id_type=MESH,
     ).wait()
 
-    for a in range(8):
-        to = row_map[0, a]
-        for k in range(4):
-            arrived[a * 4 + k] = arrived[a * 4 + k] + front_v[to * 4 + k]
-
-
-def place_kernel(row_map, summed, updated, sem):
+
+def place_kernel(row_map, arrived, partial, updated, total, sem):
     copies = []
-    for a in range(8):
-        rows = pl.ds(pl.multiple_of(row_map[0, a] * TILE, TILE), TILE)
-        copies.append(
-            pltpu.make_async_copy(
-                summed.at[a * TILE : (a + 1) * TILE], updated.at[rows], sem.at[a]
-            )
-        )
-    for copy in copies:
-        copy.start()
+    for step in range(8 * PARTS):
+        to = row_map[0, step // PARTS] * PARTS + step % PARTS
+        total[step] = arrived[step] + partial[to]
+        copies.append(pltpu.make_async_copy(total.at[step], updated.at[to], sem.at[step]))
+        copies[-1].start()
     for copy in copies:
         copy.wait()
 
@@ -332,12 +324,12 @@
     vmem = pl.BlockSpec(memory_space=pltpu.VMEM)
     hbm = pl.BlockSpec(memory_space=pltpu.HBM)
     f32 = jnp.float32
-    summed = pl.pallas_call(
+    arrived, partial = pl.pallas_call(
         exchange_kernel,
         name="exchange",
-        out_shape=jax.ShapeDtypeStruct((32, 64, 512), f32),
+        out_shape=(jax.ShapeDtypeStruct((32, 64, 512), f32),) * 2,
         in_specs=[hbm] * 13,
-        out_specs=vmem,
+        out_specs=(vmem, vmem),
         scratch_shapes=[
             pltpu.SMEM((tiles,), jnp.int32),
             pltpu.SMEM(row_map.shape, jnp.int32),
@@ -351,7 +343,6 @@
             pltpu.VMEM(dinv.shape, f32),
             pltpu.VMEM((1, TILE), jnp.int32),
             pltpu.VMEM((tiles, child.shape[0], TILE), f32),
-            pltpu.VMEM((32, 64, 512), f32),
             pltpu.VMEM((32, 64, 512), f32),
             pltpu.VMEM((32 * 64, 128), f32),
             pltpu.VMEM((8, 2, 2, 8, TILE), f32),
@@ -386,15 +377,17 @@
         pivots.reshape(1, TILE),
     )))
 
-    return pl.pallas_call(
+    cut = (8 * PARTS, TILE // PARTS, 2 * TILE)
+    updated = pl.pallas_call(
         place_kernel,
         name="place_rows",
-        out_shape=jax.ShapeDtypeStruct(front.shape, f32),
-        in_specs=[pl.BlockSpec(memory_space=pltpu.SMEM), vmem],
+        out_shape=jax.ShapeDtypeStruct(cut, f32),
+        in_specs=[pl.BlockSpec(memory_space=pltpu.SMEM), vmem, vmem],
         out_specs=hbm,
-        scratch_shapes=[pltpu.SemaphoreType.DMA((8,))],
+        scratch_shapes=[pltpu.VMEM(cut, f32), pltpu.SemaphoreType.DMA((8 * PARTS,))],
         compiler_params=pltpu.CompilerParams(vmem_limit_bytes=8 << 20),
-    )(row_map, summed.reshape(front.shape))
+    )(row_map, arrived.reshape(cut), partial.reshape(cut))
+    return updated.reshape(front.shape)
 
 
 def solution(mesh):

time: 111 us -> 110 us (level)
  no operation moved by 1% of the time
where the time goes in v3:
time: 110 us
  Pallas kernels  110 us (100%)
    pallas_call x1, Pallas kernels, on_device(): pl.pallas_call(exchange_kernel, name='exchange', out_shape=(jax.ShapeDtyp...  108 us
    pallas_call x1, Pallas kernels, on_device(): pl.pallas_call(place_kernel, name='place_rows', out_shape=jax.ShapeDtypeS...  2.7 us

profile of v3, /device:TPU:1, one launch (start us, length us, event | category | flops | bytes accessed | tf_op | source)
XLA Modules:
  0.0 110.4 jit_solution(10256762752517857592)
XLA Ops:
  0.0 0.0 copy-start
  0.0 107.7 %exchange.1 = (f32[32,64,512]{2,1,0:T(8,128)S(1)}, f32[32,64,512]{2,1,0:T(8,128)S(1)}) custom-call(s32[64]{0:T(128)} %col_map_h.1, s32[1,8]{1,0:T(1,128)} %row_map.1, s32[8]{0:T(128)} %rank_rows_h.1, s32[2]{0:T(128)} %rank_cols_h.1, s32[2,8]{1,0:T(2,128)} %bitcast.9, f32[64,16384]{1,0:T(8,128)} %child.1, f32[32,64,512]{2,1,0:T(8,128)} %bitcast.8, ...), custom_call_target="tpu_custom_call" | custom-call | tf_op jit(solution)/shard_map/exchange/pallas_call | solution.py:327
  107.7 0.0 copy-done
  107.7 2.7 %place_rows.1 = f32[16,128,512]{2,1,0:T(8,128)} custom-call(s32[1,8]{1,0:T(1,128)S(1)} %copy-done, f32[16,128,512]{2,1,0:T(8,128)S(1)} %bitcast.6, f32[16,128,512]{2,1,0:T(8,128)S(1)} %bitcast.7), custom_call_target="tpu_custom_call" | custom-call | tf_op jit(solution)/shard_map/place_rows/pallas_call | solution.py:381
Async XLA Ops:
  0.0 107.7 %copy-start = (s32[1,8]{1,0:T(1,128)S(1)}, s32[1,8]{1,0:T(1,128)}, u32[]{:S(2)}) copy-start(s32[1,8]{1,0:T(1,128)} %row_map.1) | copy-start | bytes 100

commit v4 on v3

--- a/solution.py
+++ b/solution.py
@@ -90,16 +90,12 @@
     ]
     barrier = pltpu.get_barrier_semaphore()
 
-    def greet(m, carry):
-        to = peer_of(
-            row,
-            ((z_high + m // 8) % 4) * 4 + (x + (m // 2) % 4) % 4,
-            (leaf + m % 2) % 2,
-        )
-        pl.semaphore_signal(barrier, inc=1, device_id=to, device_id_type=MESH)
-        return carry
-
-    lax.fori_loop(1, 32, greet, 0)
+    xs = [(x + step) % 4 for step in range(4)]
+    for dz in (2, 1, 3, 0):
+        plane = ((z_high + dz) % 4) * 4
+        for m in range(0 if dz else 1, 8):
+            to = peer_of(row, plane + xs[m // 2], 1 - leaf if m % 2 else leaf)
+            pl.semaphore_signal(barrier, inc=1, device_id=to, device_id_type=MESH)
     pl.semaphore_signal(
         barrier, inc=1, device_id=peer_of((1 - z_low) * 4 + y, col, leaf), device_id_type=MESH
     )
@@ -113,7 +109,7 @@
 
     for copy in small[:5]:
         copy.start()
-    lax.fori_loop(0, 64, load_tile, 0)
+    lax.fori_loop(0, 64, load_tile, 0, unroll=8)
     for copy in small[5:]:
         copy.start()
 
@@ -214,12 +210,12 @@
     settle_vz(1, 0)
     for copy in xw_x + vz_y:
         copy.start()
-    send_blocks(0, 1)
+    send_blocks(0, 3)
     settle_xw(12, 1)
     settle_vz(6, 1)
     for copy in xw_leaf:
         copy.start()
-    send_blocks(0, 3)
+    send_blocks(0, 1)
     send_blocks(1, 0)
     place_tiles(me)
     arrived[me] = out_v[me]

time: 110 us -> 110 us (level)
  no operation moved by 1% of the time
where the time goes in v4:
time: 110 us
  Pallas kernels  110 us (100%)
    pallas_call x1, Pallas kernels, on_device(): pl.pallas_call(exchange_kernel, name='exchange', out_shape=(jax.ShapeDtyp...  107 us
    pallas_call x1, Pallas kernels, on_device(): pl.pallas_call(place_kernel, name='place_rows', out_shape=jax.ShapeDtypeS...  2.7 us

profile of v4, /device:TPU:1, one launch (start us, length us, event | category | flops | bytes accessed | tf_op | source)
XLA Modules:
  0.0 109.7 jit_solution(7790523007513600373)
XLA Ops:
  0.0 0.0 copy-start
  0.0 107.0 %exchange.1 = (f32[32,64,512]{2,1,0:T(8,128)S(1)}, f32[32,64,512]{2,1,0:T(8,128)S(1)}) custom-call(s32[64]{0:T(128)} %col_map_h.1, s32[1,8]{1,0:T(1,128)} %row_map.1, s32[8]{0:T(128)} %rank_rows_h.1, s32[2]{0:T(128)} %rank_cols_h.1, s32[2,8]{1,0:T(2,128)} %bitcast.9, f32[64,16384]{1,0:T(8,128)} %child.1, f32[32,64,512]{2,1,0:T(8,128)} %bitcast.8, ...), custom_call_target="tpu_custom_call" | custom-call | tf_op jit(solution)/shard_map/exchange/pallas_call | solution.py:323
  107.0 0.0 copy-done
  107.0 2.7 %place_rows.1 = f32[16,128,512]{2,1,0:T(8,128)} custom-call(s32[1,8]{1,0:T(1,128)S(1)} %copy-done, f32[16,128,512]{2,1,0:T(8,128)S(1)} %bitcast.6, f32[16,128,512]{2,1,0:T(8,128)S(1)} %bitcast.7), custom_call_target="tpu_custom_call" | custom-call | tf_op jit(solution)/shard_map/place_rows/pallas_call | solution.py:377
Async XLA Ops:
  0.0 107.0 %copy-start = (s32[1,8]{1,0:T(1,128)S(1)}, s32[1,8]{1,0:T(1,128)}, u32[]{:S(2)}) copy-start(s32[1,8]{1,0:T(1,128)} %row_map.1) | copy-start | bytes 100

commit v5 on v4

--- a/solution.py
+++ b/solution.py
@@ -109,7 +109,7 @@
 
     for copy in small[:5]:
         copy.start()
-    lax.fori_loop(0, 64, load_tile, 0, unroll=8)
+    lax.fori_loop(0, 64, load_tile, 0, unroll=16)
     for copy in small[5:]:
         copy.start()
 

time: 110 us -> 110 us (level)
  no operation moved by 1% of the time
where the time goes in v5:
time: 110 us
  Pallas kernels  110 us (100%)
    pallas_call x1, Pallas kernels, on_device(): pl.pallas_call(exchange_kernel, name='exchange', out_shape=(jax.ShapeDtyp...  107 us
    pallas_call x1, Pallas kernels, on_device(): pl.pallas_call(place_kernel, name='place_rows', out_shape=jax.ShapeDtypeS...  2.7 us

profile of v5, /device:TPU:1, one launch (start us, length us, event | category | flops | bytes accessed | tf_op | source)
XLA Modules:
  0.0 109.7 jit_solution(9409412129607440681)
XLA Ops:
  0.0 0.0 copy-start
  0.0 107.0 %exchange.1 = (f32[32,64,512]{2,1,0:T(8,128)S(1)}, f32[32,64,512]{2,1,0:T(8,128)S(1)}) custom-call(s32[64]{0:T(128)} %col_map_h.1, s32[1,8]{1,0:T(1,128)} %row_map.1, s32[8]{0:T(128)} %rank_rows_h.1, s32[2]{0:T(128)} %rank_cols_h.1, s32[2,8]{1,0:T(2,128)} %bitcast.9, f32[64,16384]{1,0:T(8,128)} %child.1, f32[32,64,512]{2,1,0:T(8,128)} %bitcast.8, ...), custom_call_target="tpu_custom_call" | custom-call | tf_op jit(solution)/shard_map/exchange/pallas_call | solution.py:323
  107.0 0.0 copy-done
  107.0 2.7 %place_rows.1 = f32[16,128,512]{2,1,0:T(8,128)} custom-call(s32[1,8]{1,0:T(1,128)S(1)} %copy-done, f32[16,128,512]{2,1,0:T(8,128)S(1)} %bitcast.6, f32[16,128,512]{2,1,0:T(8,128)S(1)} %bitcast.7), custom_call_target="tpu_custom_call" | custom-call | tf_op jit(solution)/shard_map/place_rows/pallas_call | solution.py:377
Async XLA Ops:
  0.0 107.0 %copy-start = (s32[1,8]{1,0:T(1,128)S(1)}, s32[1,8]{1,0:T(1,128)}, u32[]{:S(2)}) copy-start(s32[1,8]{1,0:T(1,128)} %row_map.1) | copy-start | bytes 100
